TPU v7x, 512 devices: a whole 4x8x8 slice. The times are simulated.
512 devices in a mesh: wide: 64 (over y_hi, x, z), narrow: 8 (over y_lo, core).
Axes of the slice: x: 4, y: 8 (y_hi: 2, y_lo: 4; y = y_hi * 4 + y_lo), z: 8, core: 2. Of those that a mesh axis runs over, the one named last changes fastest.
Arguments:
- raw_ints: float32 [512, 512, 768], P('wide', 'narrow'), may hold values from -1.2 to 1.2
- metric: float32 [768, 768], P('narrow'), may hold values from -0.21875 to 0.21875
- occ_energy: float32 [512], P(('wide', 'narrow')), may hold values from -1.5 to -0.3
- vir_energy: float32 [512], replicated, may hold values from 0.3 to 3
- pair_kept: int32 [512], P(('wide', 'narrow')), may hold values 0 or 1
Outputs:
- density: float32 [512, 512], P('narrow')
- energy: float32 [512], P(('wide', 'narrow'))
All inputs are finite; a program needn't handle non-finite values. No bound on the sum of `pair_kept` on one device may be relied on, other than what follows from the above.
Results may differ from a plain program's by a relative error of at most 0.0003.
Values sent between devices are 32-bit elements; how exact they have to be, the bound alone decides.
A program may use at most 64 MiB of HBM per device.

v0:
```python
import jax
import jax.numpy as jnp
from jax import lax
from jax.sharding import PartitionSpec as P

HIGHEST_PRECISION = lax.Precision.HIGHEST


def passed_along(shard, axis, by):
    size = lax.axis_size(axis)
    return lax.ppermute(shard, axis, [(i, (i + by) % size) for i in range(size)])


def contract(left_block, right_block, left_dim, right_dim):
    return lax.dot_general(
        left_block,
        right_block,
        (((left_dim,), (right_dim,)), ((), ())),
        precision=HIGHEST_PRECISION,
        preferred_element_type=jnp.float32,
    )


def pair_pass(left_block, right_block, vir_energy, left_energy, right_energy):
    pair_ints = contract(left_block, right_block, 1, 1)
    denominator = vir_energy[:, None] + vir_energy[None, :] - left_energy - right_energy
    amplitude = pair_ints / denominator
    pair_value = -jnp.sum(pair_ints * (2.0 * amplitude - amplitude.T)) / (
        pair_ints.shape[0] * pair_ints.shape[1]
    )
    return (amplitude, pair_value)


def on_device(raw_ints, metric, occ_energy, vir_energy, pair_kept):
    group_size, vir_local, aux_count = raw_ints.shape
    flattened = raw_ints.reshape(group_size * vir_local, aux_count)
    fitted = contract(flattened, lax.all_gather(metric, "narrow", axis=0, tiled=True), 1, 1)
    fitted = fitted.reshape(group_size, vir_local, aux_count)
    regrouped = lax.all_to_all(fitted, "narrow", split_axis=0, concat_axis=1, tiled=True)
    own_block = regrouped[0]
    kept_mask = pair_kept.astype(jnp.float32)
    lower_block, lower_energy = passed_along((own_block, occ_energy), "wide", 1)
    amplitude, pair_value = pair_pass(
        own_block, lower_block, vir_energy, occ_energy[0], lower_energy[0]
    )
    dens_scale = 0.0625 / (lax.axis_size("wide") * lax.axis_size("narrow"))
    upper_block, upper_energy, upper_kept = passed_along(
        (own_block, occ_energy, kept_mask), "wide", -1
    )
    upper_amplitude, upper_value = pair_pass(
        own_block, upper_block, vir_energy, occ_energy[0], upper_energy[0]
    )
    energy = kept_mask * pair_value + upper_kept * upper_value
    row_term = kept_mask[0] * contract(amplitude, amplitude, 1, 1)
    row_term = row_term + upper_kept[0] * contract(upper_amplitude, upper_amplitude, 1, 1)
    partial_rows = lax.psum_scatter(
        row_term * dens_scale, "narrow", scatter_dimension=0, tiled=True
    )
    density = lax.psum(partial_rows, "wide")
    return (density, energy)


def solution(mesh):
    placed = (
        P("wide", "narrow", None),
        P("narrow", None),
        P(("wide", "narrow")),
        P(),
        P(("wide", "narrow")),
    )
    return jax.shard_map(
        on_device,
        mesh=mesh,
        in_specs=placed,
        out_specs=(P("narrow", None), P(("wide", "narrow"))),
        check_vma=False,
    )
```

profile of v0, /device:TPU:8, one launch (start us, length us, event | category | flops | bytes accessed | tf_op | source)
XLA Modules:
  0.0 1009.0 jit_solution(229166145659580155)
XLA Ops:
  7.2 0.0 copy-start
  7.2 0.0 all-gather.2.cloned.1.call-start
  7.2 0.7 all-gather.2.cloned.1.call-update
  7.9 0.0 reduce-scatter.2.cloned.1.call-start
  8.0 46.0 %all-gather.2.cloned.1.call-done = f32[768,768]{1,0:T(8,128)} async-done(((f32[96,768]{1,0:T(8,128)}), f32[768,768]{1,0:T(8,128)}) %all-gather.2.cloned.1.call-update) | async-done | bytes 2359312 | tf_op jit(solution)/shard_map/all_gather | solution.py:37
  54.0 0.0 copy-done
  54.0 5.7 fusion
  59.7 42.3 %all_to_all.4 = f32[8,64,768]{2,1,0:T(8,128)S(1)} all-to-all(f32[8,64,768]{2,1,0:T(8,128)S(1)} %fusion), channel_id=1, replica_groups=mesh['wide'=64,'narrow'=8] {'narrow'}, dimensions={0} | all-to-all | bytes 3145728 | tf_op jit(solution)/shard_map/all_to_all | solution.py:39
  102.0 11.2 %collective-permute-start.3 = (f32[512,768]{1,0:T(8,128)S(1)}, f32[512,768]{1,0:T(8,128)S(1)}, u32[]{:S(2)}, u32[]{:S(2)}) collective-permute-start(f32[512,768]{1,0:T(8,128)S(1)} %bitcast.35), channel_id=1, source_target_pairs={{0,504},{8,0},{16,8},{24,16},{32,24},{40,32},{48,40},{56,48},{64,5... | collective-permute-start | bytes 4718600 | tf_op jit(solution)/shard_map/ppermute | solution.py:11
  113.2 1.9 collective-permute-start
  115.1 1.9 collective-permute-start.1
  117.1 12.1 %collective-permute-start.4 = (f32[1]{0:T(128)}, f32[1]{0:T(128)}, u32[]{:S(2)}, u32[]{:S(2)}) collective-permute-start(f32[1]{0:T(128)} %param.7), channel_id=1, source_target_pairs={{0,504},{8,0},{16,8},{24,16},{32,24},{40,32},{48,40},{56,48},{64,5... | collective-permute-start | bytes 20 | tf_op jit(solution)/shard_map/ppermute | solution.py:11
  129.8 27.5 %collective-permute-start.2 = (f32[1]{0:T(128)}, f32[1]{0:T(128)}, u32[]{:S(2)}, u32[]{:S(2)}) collective-permute-start(f32[1]{0:T(128)} %convert_element_type.3), channel_id=1, source_target_pairs={{0,504},{8,0},{16,8},{24,16},{32,24},{40,32},{48,40},{56,48},{64,5... | collective-permute-start | bytes 20 | tf_op jit(solution)/shard_map/ppermute | solution.py:11
  157.9 0.0 copy-start.2
  157.9 0.0 collective-permute-done.3
  157.9 2.7 fusion.26
  160.6 0.0 collective-permute-done.4
  160.6 2.8 fusion.14
  163.4 6.8 collective-permute-done
  170.2 2.7 fusion.25
  172.9 0.0 collective-permute-done.1
  172.9 0.9 copy-done.1
  173.9 4.5 fusion.3
  178.4 0.0 reduce-scatter.2.cloned.1.call-update
  178.4 0.0 all-reduce.2.cloned.1.call-start
  178.5 2.6 copy.7
  181.0 1.4 copy.8
  182.4 47.7 %reduce-scatter.2.cloned.1.call-done = f32[64,512]{1,0:T(8,128)} async-done(((f32[512,512]{1,0:T(8,128)}), f32[64,512]{1,0:T(8,128)}) %reduce-scatter.2.cloned.1.call-update) | async-done | bytes 131088 | tf_op jit(solution)/shard_map/reduce_scatter | solution.py:56
  230.1 0.0 all-reduce.2.cloned.1.call-update
  230.1 4.5 fusion.13
  236.3 763.4 %all-reduce.2.cloned.1.call-done = f32[64,512]{1,0:T(8,128)} async-done(((f32[64,512]{1,0:T(8,128)}), f32[64,512]{1,0:T(8,128)}) %all-reduce.2.cloned.1.call-update) | async-done | bytes 131088 | tf_op jit(solution)/shard_map/psum | solution.py:59
  999.8 1.6 copy.12
  (3 shorter events, 0.0 us)
Async XLA Ops:
  7.2 46.8 %copy-start = (f32[8,64,768]{2,1,0:T(8,128)S(1)}, f32[8,64,768]{2,1,0:T(8,128)}, u32[]{:S(2)}) copy-start(f32[8,64,768]{2,1,0:T(8,128)} %param.5) | copy-start | bytes 4718596
  7.2 46.8 %all-gather.2.cloned.1.call-start = ((), (), s32[]{:S(2)}) async-start(), calls=%async_computation.2 | async-start | bytes 2654208 | tf_op jit(solution)/shard_map/all_gather | solution.py:37
  7.9 222.2 %reduce-scatter.2.cloned.1.call-start = ((), (), s32[]{:S(2)}) async-start(), calls=%async_computation.3 | async-start | bytes 1179648 | tf_op jit(solution)/shard_map/reduce_scatter | solution.py:56
  102.0 55.9 %collective-permute-start.3 = (f32[512,768]{1,0:T(8,128)S(1)}, f32[512,768]{1,0:T(8,128)S(1)}, u32[]{:S(2)}, u32[]{:S(2)}) collective-permute-start(f32[512,768]{1,0:T(8,128)S(1)} %bitcast.35), channel_id=1, source_target_pairs={{0,504},{8,0},{16,8},{24,16},{32,24},{40,32},{48,40},{56,48},{64,5... | collective-permute-start | bytes 4718600 | tf_op jit(solution)/shard_map/ppermute | solution.py:11
  113.2 57.0 %collective-permute-start = (f32[512,768]{1,0:T(8,128)S(1)}, f32[512,768]{1,0:T(8,128)S(1)}, u32[]{:S(2)}, u32[]{:S(2)}) collective-permute-start(f32[512,768]{1,0:T(8,128)S(1)} %bitcast.36), channel_id=1, source_target_pairs={{0,8},{8,16},{16,24},{24,32},{32,40},{40,48},{48,56},{56,64},{64,7... | collective-permute-start | bytes 4718600 | tf_op jit(solution)/shard_map/ppermute | solution.py:11
  115.1 57.8 %collective-permute-start.1 = (f32[1]{0:T(128)}, f32[1]{0:T(128)}, u32[]{:S(2)}, u32[]{:S(2)}) collective-permute-start(f32[1]{0:T(128)} %param.7), channel_id=1, source_target_pairs={{0,8},{8,16},{16,24},{24,32},{32,40},{40,48},{48,56},{56,64},{64,7... | collective-permute-start | bytes 20 | tf_op jit(solution)/shard_map/ppermute | solution.py:11
  117.1 43.5 %collective-permute-start.4 = (f32[1]{0:T(128)}, f32[1]{0:T(128)}, u32[]{:S(2)}, u32[]{:S(2)}) collective-permute-start(f32[1]{0:T(128)} %param.7), channel_id=1, source_target_pairs={{0,504},{8,0},{16,8},{24,16},{32,24},{40,32},{48,40},{56,48},{64,5... | collective-permute-start | bytes 20 | tf_op jit(solution)/shard_map/ppermute | solution.py:11
  129.8 43.1 %collective-permute-start.2 = (f32[1]{0:T(128)}, f32[1]{0:T(128)}, u32[]{:S(2)}, u32[]{:S(2)}) collective-permute-start(f32[1]{0:T(128)} %convert_element_type.3), channel_id=1, source_target_pairs={{0,504},{8,0},{16,8},{24,16},{32,24},{40,32},{48,40},{56,48},{64,5... | collective-permute-start | bytes 20 | tf_op jit(solution)/shard_map/ppermute | solution.py:11
  157.9 2.7 copy-start.2
  172.9 1.0 copy-start.1
  178.4 821.3 %all-reduce.2.cloned.1.call-start = ((), (), s32[]{:S(2)}) async-start(), calls=%async_computation.4 | async-start | bytes 262144 | tf_op jit(solution)/shard_map/psum | solution.py:59
Sparse Core Ops, SparseCore 0:
  10.1 43.8 all-gather.1
  178.5 51.4 reduce-scatter.1
  233.0 766.7 all-reduce.1
where the time goes:
time: 1010 us
  waiting for transfers between devices  865 us (86%)
  starting transfers between devices  54.7 us (5%)
  blocking collectives  42.3 us (4%)
  matrix products  18.4 us (2%)
  between operations  18 us (2%)
    psum x1, waiting for transfers between devices, on_device(): density = lax.psum(partial_rows, 'wide')  763 us
    ppermute x5, starting transfers between devices, passed_along(): lax.ppermute(shard, axis, [(i, (i + by) % size) for i in range(size)])  54.6 us
    reduce_scatter x1, waiting for transfers between devices, on_device(): lax.psum_scatter(row_term * dens_scale, 'narrow', scatter_dimension=0, ti...  47.7 us
    all_gather x1, waiting for transfers between devices, on_device(): lax.all_gather(metric, 'narrow', axis=0, tiled=True)  46 us
    all_to_all x1, blocking collectives, on_device(): lax.all_to_all(fitted, 'narrow', split_axis=0, concat_axis=1, tiled=True)  42.3 us
  transfers between devices with their start and end apart: 8, of which 4 were waited for; matrix products, arithmetic and copies ran while one was open for 2% of the time, Pallas kernels for 0%

commit v1 on v0

v1 whole, which is shorter than its diff:
```python
import functools

import jax
import jax.numpy as jnp
from jax import lax
from jax.experimental import pallas as pl
from jax.experimental.pallas import tpu as pltpu
from jax.sharding import PartitionSpec as P

MESH = pl.DeviceIdType.MESH
F32 = jnp.float32
BF16 = jnp.bfloat16

NX, NZ, NY, NARROW = 4, 8, 4, 8
PLANE = NX * NZ


def split(value):
    high = value.astype(BF16)
    return high, (value - high.astype(F32)).astype(BF16)


def dot_nt(left, right):
    return lax.dot_general(left, right, (((1,), (1,)), ((), ())), preferred_element_type=F32)


def dot3(left_hi, left_lo, right_hi, right_lo):
    return dot_nt(left_hi, right_hi) + (dot_nt(left_hi, right_lo) + dot_nt(left_lo, right_hi))


def kernel(
    n_wide, dens_scale,
    raw, metric, side, vir,
    dens_out, energy_out,
    rbuf, jbuf, mbuf, m_hi, m_lo, x_hi, x_lo, fi_hi, fi_lo, fj_hi, fj_lo,
    rinv, pbuf, abuf, c_hi, c_lo, dbuf, dpart, s0, xbuf, s1, zbuf, s2, ybuf, tbuf, ofull,
    side_in, pv_own, pv_in,
    loc_sem, a_s, a_r, f_s, f_r, m1_s, m1_r, m2_s, m2_r, m3_s, m3_r, side_sem, pv_sem,
    c_s, c_r, xs_s, xs_r, zs_s, zs_r, ys_s, ys_r, gz_s, gz_r, gx_s, gx_r,
):
    w = lax.axis_index("wide")
    n = lax.axis_index("narrow")
    y, c = n // 2, n % 2
    hi, plane = w // PLANE, w % PLANE
    x, z = plane // NZ, plane % NZ
    gy = hi * NY + y
    up = (w + 1) % n_wide
    down = (w + n_wide - 1) % n_wide
    fwd = (w + 1 - 2 * c + n_wide) % n_wide
    back = (w - 1 + 2 * c + n_wide) % n_wide

    def remote(src, dst, ss, rs, wide, narrow):
        return pltpu.make_async_remote_copy(
            src_ref=src, dst_ref=dst, send_sem=ss, recv_sem=rs,
            device_id=(wide, narrow), device_id_type=MESH,
        )

    def at_x(d):
        return hi * PLANE + ((x + d) % NX) * NZ + z

    def at_z(d):
        return hi * PLANE + x * NZ + (z + d) % NZ

    def at_y(d):
        there = (gy + d) % (2 * NY)
        return (there // NY) * PLANE + plane, 2 * (there % NY) + c

    peers = [(w, (n + d) % NARROW) for d in range(1, NARROW)]
    peers += [at_y(d) for d in range(1, 2 * NY)]
    peers += [(at_x(d), n) for d in range(1, NX)]
    peers += [(at_z(d), n) for d in range(1, NZ)]
    peers += [(up, n), (down, n)]
    barrier = pltpu.get_barrier_semaphore()
    for peer in peers:
        pl.semaphore_signal(barrier, inc=1, device_id=peer, device_id_type=MESH)
    pl.semaphore_wait(barrier, len(peers))

    rows_q = metric.shape[0] // NX
    own_rows = pl.ds(x * (NY * rows_q) + y * rows_q, rows_q)
    m1 = []
    for d in range(1, NY):
        copy = remote(
            metric.at[pl.ds(x * rows_q, rows_q)], mbuf.at[own_rows],
            m1_s.at[d], m1_r.at[d], w, 2 * ((y + d) % NY) + c,
        )
        copy.start()
        m1.append(copy)
    m_local = pltpu.make_async_copy(metric.at[pl.ds(x * rows_q, rows_q)], mbuf.at[own_rows], loc_sem.at[0])
    m_local.start()
    side_copy = remote(side, side_in, side_sem.at[0], side_sem.at[1], fwd, n)
    side_copy.start()

    a2a = [None]
    for d in range(1, NARROW):
        to = (n + d) % NARROW
        copy = remote(raw.at[to], rbuf.at[n], a_s.at[d], a_r.at[d], w, to)
        copy.start()
        a2a.append(copy)
    own_slot = pltpu.make_async_copy(raw.at[n], rbuf.at[n], loc_sem.at[1])
    own_slot.start()
    slots = [(n + NARROW - d) % NARROW for d in range(NARROW)]
    forwards = []

    def forward(d):
        src = raw.at[n] if d == 0 else rbuf.at[slots[d]]
        copy = remote(src, jbuf.at[slots[d]], f_s.at[d], f_r.at[d], fwd, n)
        copy.start()
        forwards.append(copy)

    forward(0)
    a2a[1].wait_recv()
    forward(1)

    m_local.wait()
    for copy in m1:
        copy.wait_recv()
    block = NY * rows_q
    half = NX * block
    m2 = []
    for d in range(1, NX):
        rows = pl.ds(x * block, block)
        copy = remote(mbuf.at[rows], mbuf.at[rows], m2_s.at[d], m2_r.at[d], at_x(d), n)
        copy.start()
        m2.append(copy)
    m3 = []

    def to_partner(d):
        which = (x + NX - d) % NX
        copy = remote(
            mbuf.at[pl.ds(which * block, block)], mbuf.at[pl.ds(half + which * block, block)],
            m3_s.at[d], m3_r.at[d], w, 2 * y + 1 - c,
        )
        copy.start()
        m3.append(copy)

    to_partner(0)

    side_copy.wait()
    virtuals = vir.shape[1]
    rinv[...] = jnp.broadcast_to(vir[...], (virtuals, virtuals))
    energies = side[0][:1, :1] + side_in[0][:1, :1]
    for r in range(0, virtuals, 128):
        across = rinv[:, r:r + 128].T
        pbuf[r:r + 128, :] = 1.0 / ((rinv[r:r + 128, :] + across) - energies)

    a2a[2].wait_recv()
    forward(2)
    a2a[3].wait_recv()
    forward(3)
    for d in range(1, NX):
        m2[d - 1].wait_recv()
        to_partner(d)
    a2a[4].wait_recv()
    forward(4)
    for copy in m3:
        copy.wait_recv()

    def split_rows(k, carry):
        rows = pl.ds(pl.multiple_of(k * 96, 96), 96)
        m_hi[rows, :], m_lo[rows, :] = split(mbuf[rows, :])
        return carry

    lax.fori_loop(0, mbuf.shape[0] // 96, split_rows, 0)

    def fit(src, f_hi, f_lo, four):
        for k, slot in enumerate(four):
            part = pl.ds(k * 64, 64)
            x_hi[part, :], x_lo[part, :] = split(src[slot])

        def tile(t, carry):
            cols = pl.ds(pl.multiple_of(t * 256, 256), 256)
            fitted = dot3(x_hi[...], x_lo[...], m_hi[cols, :], m_lo[cols, :])
            high, low = split(fitted)
            for k, slot in enumerate(four):
                f_hi[slot, :, cols] = high[k * 64:(k + 1) * 64]
                f_lo[slot, :, cols] = low[k * 64:(k + 1) * 64]
            return carry

        lax.fori_loop(0, mbuf.shape[0] // 256, tile, 0)

    own_slot.wait()
    fit(rbuf, fi_hi, fi_lo, slots[:4])
    a2a[5].wait_recv()
    forward(5)
    for d in range(4):
        forwards[d].wait_recv()
    fit(jbuf, fj_hi, fj_lo, slots[:4])
    a2a[6].wait_recv()
    forward(6)
    a2a[7].wait_recv()
    forward(7)
    fit(rbuf, fi_hi, fi_lo, slots[4:])
    for d in range(4, 8):
        forwards[d].wait_recv()
    fit(jbuf, fj_hi, fj_lo, slots[4:])

    rinv[...] = pbuf[...]

    def pair_tile(t, carry):
        ra, cb = t // 2, t % 2
        four_a, four_b = pl.ds(ra * 4, 4), pl.ds(cb * 4, 4)
        shape = (256, fi_hi.shape[2])
        ints = dot3(
            fi_hi[four_a].reshape(shape), fi_lo[four_a].reshape(shape),
            fj_hi[four_b].reshape(shape), fj_lo[four_b].reshape(shape),
        )
        rows = pl.ds(pl.multiple_of(ra * 256, 256), 256)
        cols = pl.ds(pl.multiple_of(cb * 256, 256), 256)
        pbuf[rows, cols] = ints
        abuf[rows, cols] = ints * rinv[rows, cols]
        return carry

    lax.fori_loop(0, 4, pair_tile, 0)

    def value_tile(t, total):
        ra, cb = t // 2, t % 2
        rows = pl.ds(pl.multiple_of(ra * 256, 256), 256)
        cols = pl.ds(pl.multiple_of(cb * 256, 256), 256)
        cols_t = pl.ds(pl.multiple_of(virtuals + cb * 256, 256), 256)
        amp = abuf[rows, cols]
        amp_t = abuf[cols, rows].T
        c_hi[rows, cols], c_lo[rows, cols] = split(amp)
        c_hi[rows, cols_t], c_lo[rows, cols_t] = split(amp_t)
        return total + jnp.sum(pbuf[rows, cols] * (2.0 * amp - amp_t), axis=0, keepdims=True)

    total = lax.fori_loop(0, 4, value_tile, jnp.zeros((1, 256), F32))
    kept = jnp.where(c == 0, side[1], side_in[1])
    pair_sum = jnp.sum(total, axis=1, keepdims=True)
    pv_own[...] = -kept * (jnp.broadcast_to(pair_sum, kept.shape) / (virtuals * virtuals))
    pv_copy = remote(pv_own, pv_in, pv_sem.at[0], pv_sem.at[1], back, n)
    pv_copy.start()

    scale = kept[:1, :1] * dens_scale

    def dens_tile(t, carry):
        ra, cb = t // 2, t % 2
        rows = pl.ds(pl.multiple_of(ra * 256, 256), 256)
        cols = pl.ds(pl.multiple_of(cb * 256, 256), 256)
        dens = dot3(c_hi[rows, :], c_lo[rows, :], c_hi[cols, :], c_lo[cols, :]) * scale
        for k in range(4):
            for q in range(NX):
                start = k * 64 + q * 16
                dbuf[k % 2, q, ra * 2 + k // 2, :, cols] = dens[start:start + 16]
        return carry

    lax.fori_loop(0, 4, dens_tile, 0)

    core_copies = []
    for d in (1, 2, 3, 0):
        q = (x + d) % NX
        copy = remote(dbuf.at[1 - c, q], dpart.at[q], c_s.at[d], c_r.at[d], w, 2 * y + 1 - c)
        copy.start()
        core_copies.append(copy)
    x_copies = []
    for copy, d in zip(core_copies, (1, 2, 3, 0)):
        q = (x + d) % NX
        copy.wait_recv()
        s0[q] = dbuf[c, q] + dpart[q]
        if d:
            out = remote(s0.at[q], xbuf.at[d], xs_s.at[d], xs_r.at[d], at_x(d), n)
            out.start()
            x_copies.append(out)
    for copy in x_copies:
        copy.wait_recv()
    sum_x = ((s0[x] + xbuf[1]) + xbuf[2]) + xbuf[3]
    for k in range(NZ):
        r, q = k // 4, k % 4
        s1[k] = sum_x[:, r * 8:r * 8 + 8, q * 128:q * 128 + 128]

    z_copies = []
    for d in range(1, NZ):
        copy = remote(s1.at[(z + d) % NZ], zbuf.at[d], zs_s.at[d], zs_r.at[d], at_z(d), n)
        copy.start()
        z_copies.append(copy)
    for copy in z_copies:
        copy.wait_recv()
    sum_z = s1[z]
    for d in range(1, NZ):
        sum_z = sum_z + zbuf[d]
    s2[...] = sum_z

    y_copies = []
    for d in range(1, 2 * NY):
        wide, narrow = at_y(d)
        copy = remote(s2.at[(y + d) % NY], ybuf.at[gy], ys_s.at[d], ys_r.at[d], wide, narrow)
        copy.start()
        y_copies.append(copy)
    ybuf[gy] = s2[y]
    for copy in y_copies:
        copy.wait_recv()
    sum_y = ybuf[0]
    for k in range(1, 2 * NY):
        sum_y = sum_y + ybuf[k]
    tbuf[...] = sum_y

    rows = pl.ds(pl.multiple_of(x * 16 + (z // 4) * 8, 8), 8)
    cols = pl.ds(pl.multiple_of((z % 4) * 128, 128), 128)
    gz = []
    for d in range(1, NZ):
        copy = remote(tbuf, ofull.at[rows, cols], gz_s.at[d], gz_r.at[d], at_z(d), n)
        copy.start()
        gz.append(copy)
    ofull[rows, cols] = sum_y
    for copy in gz:
        copy.wait_recv()
    rows = pl.ds(pl.multiple_of(x * 16, 16), 16)
    gx = []
    for d in range(1, NX):
        copy = remote(ofull.at[rows], ofull.at[rows], gx_s.at[d], gx_r.at[d], at_x(d), n)
        copy.start()
        gx.append(copy)
    pv_copy.wait()
    energy_out[...] = pv_own[...] + pv_in[...]
    for copy in gx:
        copy.wait_recv()
    dens_out[...] = ofull[...]

    for copy in m1 + m2 + m3 + a2a[1:] + forwards + core_copies + x_copies + z_copies + y_copies + gz + gx:
        copy.wait_send()


def on_device(n_wide, raw_ints, metric, occ_energy, vir_energy, pair_kept):
    orbitals, vir_local, aux = raw_ints.shape
    virtuals = vir_energy.shape[0]
    dens_scale = 0.0625 / (n_wide * NARROW)
    side = jnp.stack([occ_energy, pair_kept.astype(F32)])[:, :, None]
    side = jnp.broadcast_to(side, (2, 8, 128))
    dma = pltpu.SemaphoreType.DMA
    vmem = pltpu.VMEM
    fit_shape = (orbitals, vir_local, aux)
    scratch = [
        vmem(fit_shape, F32), vmem(fit_shape, F32), vmem((aux, aux), F32),
        vmem((aux, aux), BF16), vmem((aux, aux), BF16),
        vmem((256, aux), BF16), vmem((256, aux), BF16),
        vmem(fit_shape, BF16), vmem(fit_shape, BF16), vmem(fit_shape, BF16), vmem(fit_shape, BF16),
        vmem((virtuals, virtuals), F32), vmem((virtuals, virtuals), F32), vmem((virtuals, virtuals), F32),
        vmem((virtuals, 2 * virtuals), BF16), vmem((virtuals, 2 * virtuals), BF16),
        vmem((2, NX, NY, 16, virtuals), F32), vmem((NX, NY, 16, virtuals), F32), vmem((NX, NY, 16, virtuals), F32),
        vmem((NX, NY, 16, virtuals), F32),
        vmem((NZ, NY, 8, 128), F32), vmem((NZ, NY, 8, 128), F32), vmem((NY, 8, 128), F32),
        vmem((2 * NY, 8, 128), F32), vmem((8, 128), F32), vmem((vir_local, virtuals), F32),
        vmem((2, 8, 128), F32), vmem((8, 128), F32), vmem((8, 128), F32),
        dma((2,)), dma((8,)), dma((8,)), dma((8,)), dma((8,)),
        dma((4,)), dma((4,)), dma((4,)), dma((4,)), dma((4,)), dma((4,)), dma((2,)), dma((2,)),
        dma((4,)), dma((4,)), dma((4,)), dma((4,)), dma((8,)), dma((8,)), dma((8,)), dma((8,)),
        dma((8,)), dma((8,)), dma((4,)), dma((4,)),
    ]
    any_space = pl.BlockSpec(memory_space=pl.ANY)
    in_vmem = pl.BlockSpec(memory_space=pltpu.VMEM)
    density, energy = pl.pallas_call(
        functools.partial(kernel, n_wide, dens_scale),
        out_shape=(
            jax.ShapeDtypeStruct((vir_local, virtuals), F32),
            jax.ShapeDtypeStruct((8, 128), F32),
        ),
        in_specs=[any_space, any_space, in_vmem, in_vmem],
        out_specs=(in_vmem, in_vmem),
        scratch_shapes=scratch,
        compiler_params=pltpu.CompilerParams(
            collective_id=0, has_side_effects=True, vmem_limit_bytes=48 << 20
        ),
        name="pair_density",
    )(raw_ints, metric, side, vir_energy[None, :])
    return density, energy[0, :1]


def solution(mesh):
    placed = (
        P("wide", "narrow", None),
        P("narrow", None),
        P(("wide", "narrow")),
        P(),
        P(("wide", "narrow")),
    )
    return jax.shard_map(
        functools.partial(on_device, mesh.shape["wide"]),
        mesh=mesh,
        in_specs=placed,
        out_specs=(P("narrow", None), P(("wide", "narrow"))),
        check_vma=False,
    )
```

time: 1010 us -> 138 us (0.14)
  waiting for transfers between devices: 865 us -> 0 us
  Pallas kernels: 0 us -> 132 us
  starting transfers between devices: 54.7 us -> 0 us
  blocking collectives: 42.3 us -> 0 us
  matrix products: 18.4 us -> 0 us
  between operations: 18 us -> 1.93 us
    psum x1 -> x0, waiting for transfers between devices: 763 us -> none  [on_device(): density = lax.psum(partial_rows, 'wide')]
    pallas_call x0 -> x1, Pallas kernels: none -> 132 us  [on_device(): pl.pallas_call(functools.partial(kernel, n_wide, dens_scale), out_shape=(...]
    ppermute x5 -> x0, starting transfers between devices: 54.6 us -> none  [passed_along(): lax.ppermute(shard, axis, [(i, (i + by) % size) for i in range(size)])]
    reduce_scatter x1 -> x0, waiting for transfers between devices: 47.7 us -> none  [on_device(): lax.psum_scatter(row_term * dens_scale, 'narrow', scatter_dimension=0, ti...]
    all_gather x1 -> x0, waiting for transfers between devices: 46 us -> none  [on_device(): lax.all_gather(metric, 'narrow', axis=0, tiled=True)]
    all_to_all x1 -> x0, blocking collectives: 42.3 us -> none  [on_device(): lax.all_to_all(fitted, 'narrow', split_axis=0, concat_axis=1, tiled=True)]
    dot_general x5 -> x0, matrix products: 18.4 us -> none  [contract(): lax.dot_general(left_block, right_block, (((left_dim,), (right_dim,)), ((...]
  transfers between devices with their start and end apart: 8 -> 0, of which waited for: 4 -> 0; matrix products, arithmetic and copies ran while one was open for 2% -> 0% of each run, Pallas kernels for 0% -> 0%
where the time goes in v1:
time: 138 us
  Pallas kernels  132 us (96%)
  local copies, waits for them, and re-layouts  4.29 us (3%)
  between operations  1.93 us (1%)
    pallas_call x1, Pallas kernels, on_device(): pl.pallas_call(functools.partial(kernel, n_wide, dens_scale), out_shape=(...  132 us
    unnamed x7, local copies, waits for them, and re-layouts  3.71 us

profile of v1, /device:TPU:8, one launch (start us, length us, event | category | flops | bytes accessed | tf_op | source)
XLA Modules:
  0.0 137.8 jit_solution(8176134535446115600)
XLA Ops:
  1.9 0.1 maximum_bitcast_fusion
  2.0 0.1 broadcast_in_dim.12.side
  2.1 0.0 copy-start
  2.1 1.4 %copy-done = f32[8,64,768]{2,1,0:T(8,128)S(1)} copy-done((f32[8,64,768]{2,1,0:T(8,128)S(1)}, f32[8,64,768]{2,1,0:T(8,128)}, u32[]{:S(2)}) %copy-start) | copy-done | bytes 1572888
  3.5 0.0 copy-start.1
  3.5 1.0 copy-done.1
  4.4 0.0 copy-start.2
  4.4 0.7 copy-done.2
  5.1 131.5 %pair_density.1 = (f32[64,512]{1,0:T(8,128)S(1)}, f32[8,128]{1,0:T(8,128)S(1)}) custom-call(f32[8,64,768]{2,1,0:T(8,128)S(1)} %copy-done, f32[96,768]{1,0:T(8,128)S(1)} %copy-done.1, f32[2,8,128]{2,1,0:T(8,128)S(1)} %broadcast_in_dim.12.side, f32[1,512]{1,0:T(1,128)S(1)} %bitcast.7), custom_call_target="tpu_custom_call" | custom-call | tf_op jit(solution)/shard_map/pair_density/pallas_call | solution.py:350
  136.7 0.5 slice.3
  137.2 0.7 copy.10
Async XLA Ops:
  2.1 1.4 %copy-start = (f32[8,64,768]{2,1,0:T(8,128)S(1)}, f32[8,64,768]{2,1,0:T(8,128)}, u32[]{:S(2)}) copy-start(f32[8,64,768]{2,1,0:T(8,128)} %raw.1) | copy-start | bytes 4718596
  3.5 1.0 copy-start.1
  4.4 0.7 copy-start.2

commit v2 on v1

--- a/solution.py
+++ b/solution.py
@@ -13,6 +13,9 @@
 
 NX, NZ, NY, NARROW = 4, 8, 4, 8
 PLANE = NX * NZ
+LAST, FIRST = PLANE - 1, 0
+UP_COLUMNS = (24, 7, 25, 6)
+DOWN_COLUMNS = (23, 8, 16, 15)
 
 
 def split(value):
@@ -35,6 +38,7 @@
     rbuf, jbuf, mbuf, m_hi, m_lo, x_hi, x_lo, fi_hi, fi_lo, fj_hi, fj_lo,
     rinv, pbuf, abuf, c_hi, c_lo, dbuf, dpart, s0, xbuf, s1, zbuf, s2, ybuf, tbuf, ofull,
     side_in, pv_own, pv_in,
+    relay_buf, b_s, b_r, r_s,
     loc_sem, a_s, a_r, f_s, f_r, m1_s, m1_r, m2_s, m2_r, m3_s, m3_r, side_sem, pv_sem,
     c_s, c_r, xs_s, xs_r, zs_s, zs_r, ys_s, ys_r, gz_s, gz_r, gx_s, gx_r,
 ):
@@ -71,9 +75,45 @@
     peers += [(at_z(d), n) for d in range(1, NZ)]
     peers += [(up, n), (down, n)]
     barrier = pltpu.get_barrier_semaphore()
+
+    def greet(wide, narrow):
+        pl.semaphore_signal(barrier, inc=1, device_id=(wide, narrow), device_id_type=MESH)
+
     for peer in peers:
-        pl.semaphore_signal(barrier, inc=1, device_id=peer, device_id_type=MESH)
-    pl.semaphore_wait(barrier, len(peers))
+        greet(*peer)
+    routes = ((LAST, FIRST, 0, UP_COLUMNS), (FIRST, LAST, 1, DOWN_COLUMNS))
+    sends_on = jnp.logical_not(((plane == LAST) & (c == 0)) | ((plane == FIRST) & (c == 1)))
+    for source, target, parity, columns in routes:
+        @pl.when(plane == source)
+        def _():
+            for column in columns:
+                greet(hi * PLANE + column, n)
+
+        for j, column in enumerate(columns):
+            @pl.when(plane == column)
+            def _():
+                greet(hi * PLANE + source, n)
+                greet((1 - hi) * PLANE + target, 2 * ((j + NY - y) % NY) + parity)
+
+        @pl.when((plane == target) & (c == parity))
+        def _():
+            for j, column in enumerate(columns):
+                for core in range(2):
+                    greet((1 - hi) * PLANE + column, 2 * ((j + NY - y) % NY) + core)
+
+    at_end = (plane == LAST) | (plane == FIRST)
+    on_way = plane == UP_COLUMNS[0]
+    for column in UP_COLUMNS[1:] + DOWN_COLUMNS:
+        on_way = on_way | (plane == column)
+    for case, more in (
+        (at_end & sends_on, 3 * len(UP_COLUMNS)),
+        (at_end & jnp.logical_not(sends_on), len(UP_COLUMNS)),
+        (on_way, 2),
+        (jnp.logical_not(at_end | on_way), 0),
+    ):
+        @pl.when(case)
+        def _():
+            pl.semaphore_wait(barrier, len(peers) + more)
 
     rows_q = metric.shape[0] // NX
     own_rows = pl.ds(x * (NY * rows_q) + y * rows_q, rows_q)
@@ -90,6 +130,15 @@
     side_copy = remote(side, side_in, side_sem.at[0], side_sem.at[1], fwd, n)
     side_copy.start()
 
+    for source, target, parity, columns in routes:
+        @pl.when(plane == source)
+        def _():
+            for j, column in enumerate(columns):
+                k = (j + NY - y) % NY
+                remote(
+                    raw.at[2 * k + parity], relay_buf, b_s.at[j], b_r.at[0], hi * PLANE + column, n
+                ).start()
+
     a2a = [None]
     for d in range(1, NARROW):
         to = (n + d) % NARROW
@@ -104,12 +153,28 @@
     def forward(d):
         src = raw.at[n] if d == 0 else rbuf.at[slots[d]]
         copy = remote(src, jbuf.at[slots[d]], f_s.at[d], f_r.at[d], fwd, n)
-        copy.start()
         forwards.append(copy)
+
+        @pl.when(sends_on)
+        def _():
+            copy.start()
 
     forward(0)
     a2a[1].wait_recv()
     forward(1)
+
+    def second_leg(target, parity, j):
+        to = 2 * ((j + NY - y) % NY) + parity
+        return remote(
+            relay_buf, jbuf.at[n], r_s.at[0], f_r.at[(to + NARROW - n) % NARROW], (1 - hi) * PLANE + target, to
+        )
+
+    for source, target, parity, columns in routes:
+        for j, column in enumerate(columns):
+            @pl.when(plane == column)
+            def _():
+                remote(raw.at[0], relay_buf, b_s.at[j], b_r.at[0], hi * PLANE + source, n).wait_recv()
+                second_leg(target, parity, j).start()
 
     m_local.wait()
     for copy in m1:
@@ -143,15 +208,14 @@
         across = rinv[:, r:r + 128].T
         pbuf[r:r + 128, :] = 1.0 / ((rinv[r:r + 128, :] + across) - energies)
 
-    a2a[2].wait_recv()
-    forward(2)
-    a2a[3].wait_recv()
-    forward(3)
+    for d in (2, 3, 4):
+        a2a[d].wait_recv()
+        forward(d)
     for d in range(1, NX):
         m2[d - 1].wait_recv()
         to_partner(d)
-    a2a[4].wait_recv()
-    forward(4)
+    a2a[5].wait_recv()
+    forward(5)
     for copy in m3:
         copy.wait_recv()
 
@@ -178,18 +242,15 @@
 
         lax.fori_loop(0, mbuf.shape[0] // 256, tile, 0)
 
+    for d in (6, 7):
+        a2a[d].wait_recv()
+        forward(d)
     own_slot.wait()
     fit(rbuf, fi_hi, fi_lo, slots[:4])
-    a2a[5].wait_recv()
-    forward(5)
+    fit(rbuf, fi_hi, fi_lo, slots[4:])
     for d in range(4):
         forwards[d].wait_recv()
     fit(jbuf, fj_hi, fj_lo, slots[:4])
-    a2a[6].wait_recv()
-    forward(6)
-    a2a[7].wait_recv()
-    forward(7)
-    fit(rbuf, fi_hi, fi_lo, slots[4:])
     for d in range(4, 8):
         forwards[d].wait_recv()
     fit(jbuf, fj_hi, fj_lo, slots[4:])
@@ -232,40 +293,41 @@
 
     scale = kept[:1, :1] * dens_scale
 
-    def dens_tile(t, carry):
-        ra, cb = t // 2, t % 2
-        rows = pl.ds(pl.multiple_of(ra * 256, 256), 256)
-        cols = pl.ds(pl.multiple_of(cb * 256, 256), 256)
-        dens = dot3(c_hi[rows, :], c_lo[rows, :], c_hi[cols, :], c_lo[cols, :]) * scale
-        for k in range(4):
-            for q in range(NX):
-                start = k * 64 + q * 16
-                dbuf[k % 2, q, ra * 2 + k // 2, :, cols] = dens[start:start + 16]
-        return carry
-
-    lax.fori_loop(0, 4, dens_tile, 0)
-
-    core_copies = []
-    for d in (1, 2, 3, 0):
-        q = (x + d) % NX
-        copy = remote(dbuf.at[1 - c, q], dpart.at[q], c_s.at[d], c_r.at[d], w, 2 * y + 1 - c)
-        copy.start()
-        core_copies.append(copy)
+    core_copies = [None] * NX
+    quarters = [((x // 2 + 1 + d // 2) % 2) * 2 + (x + d + d // 2) % 2 for d in range(NX)]
+    for d in range(NX):
+        q = quarters[d]
+        if d % 2 == 0:
+            half_cols = q // 2
+
+            def dens_tile(ra, carry):
+                rows = pl.ds(pl.multiple_of(ra * 256, 256), 256)
+                cols = pl.ds(pl.multiple_of(half_cols * 256, 256), 256)
+                dens = dot3(c_hi[rows, :], c_lo[rows, :], c_hi[cols, :], c_lo[cols, :]) * scale
+                for k in range(4):
+                    for e in range(2):
+                        dbuf[half_cols * 2 + e, k % 2, ra * 2 + k // 2] = dens[k * 64:k * 64 + 64, e * 128:e * 128 + 128]
+                return carry
+
+            lax.fori_loop(0, 2, dens_tile, 0)
+        copy = remote(dbuf.at[q, 1 - c], dpart.at[q], c_s.at[d], c_r.at[d], w, 2 * y + 1 - c)
+        copy.start()
+        core_copies[d] = copy
     x_copies = []
-    for copy, d in zip(core_copies, (1, 2, 3, 0)):
-        q = (x + d) % NX
-        copy.wait_recv()
-        s0[q] = dbuf[c, q] + dpart[q]
-        if d:
-            out = remote(s0.at[q], xbuf.at[d], xs_s.at[d], xs_r.at[d], at_x(d), n)
+    for copy, d in zip(core_copies, range(NX)):
+        q = quarters[d]
+        copy.wait_recv()
+        s0[q] = dbuf[q, c] + dpart[q]
+        if d < NX - 1:
+            out = remote(s0.at[q], xbuf.at[x], xs_s.at[d], xs_r.at[d], hi * PLANE + q * NZ + z, n)
             out.start()
             x_copies.append(out)
     for copy in x_copies:
         copy.wait_recv()
-    sum_x = ((s0[x] + xbuf[1]) + xbuf[2]) + xbuf[3]
+    xbuf[x] = s0[x]
+    sum_x = ((xbuf[0] + xbuf[1]) + xbuf[2]) + xbuf[3]
     for k in range(NZ):
-        r, q = k // 4, k % 4
-        s1[k] = sum_x[:, r * 8:r * 8 + 8, q * 128:q * 128 + 128]
+        s1[k] = sum_x[:, k * 8:k * 8 + 8, :]
 
     z_copies = []
     for d in range(1, NZ):
@@ -293,8 +355,8 @@
         sum_y = sum_y + ybuf[k]
     tbuf[...] = sum_y
 
-    rows = pl.ds(pl.multiple_of(x * 16 + (z // 4) * 8, 8), 8)
-    cols = pl.ds(pl.multiple_of((z % 4) * 128, 128), 128)
+    rows = pl.ds(pl.multiple_of(z * 8, 8), 8)
+    cols = pl.ds(pl.multiple_of(x * 128, 128), 128)
     gz = []
     for d in range(1, NZ):
         copy = remote(tbuf, ofull.at[rows, cols], gz_s.at[d], gz_r.at[d], at_z(d), n)
@@ -303,10 +365,9 @@
     ofull[rows, cols] = sum_y
     for copy in gz:
         copy.wait_recv()
-    rows = pl.ds(pl.multiple_of(x * 16, 16), 16)
     gx = []
     for d in range(1, NX):
-        copy = remote(ofull.at[rows], ofull.at[rows], gx_s.at[d], gx_r.at[d], at_x(d), n)
+        copy = remote(ofull.at[:, cols], ofull.at[:, cols], gx_s.at[d], gx_r.at[d], at_x(d), n)
         copy.start()
         gx.append(copy)
     pv_copy.wait()
@@ -315,7 +376,23 @@
         copy.wait_recv()
     dens_out[...] = ofull[...]
 
-    for copy in m1 + m2 + m3 + a2a[1:] + forwards + core_copies + x_copies + z_copies + y_copies + gz + gx:
+    for source, target, parity, columns in routes:
+        @pl.when(plane == source)
+        def _():
+            for j, column in enumerate(columns):
+                remote(raw.at[0], relay_buf, b_s.at[j], b_r.at[0], hi * PLANE + column, n).wait_send()
+
+        for j, column in enumerate(columns):
+            @pl.when(plane == column)
+            def _():
+                second_leg(target, parity, j).wait_send()
+
+    @pl.when(sends_on)
+    def _():
+        for copy in forwards:
+            copy.wait_send()
+
+    for copy in m1 + m2 + m3 + a2a[1:] + core_copies + x_copies + z_copies + y_copies + gz + gx:
         copy.wait_send()
 
 
@@ -335,17 +412,18 @@
         vmem(fit_shape, BF16), vmem(fit_shape, BF16), vmem(fit_shape, BF16), vmem(fit_shape, BF16),
         vmem((virtuals, virtuals), F32), vmem((virtuals, virtuals), F32), vmem((virtuals, virtuals), F32),
         vmem((virtuals, 2 * virtuals), BF16), vmem((virtuals, 2 * virtuals), BF16),
-        vmem((2, NX, NY, 16, virtuals), F32), vmem((NX, NY, 16, virtuals), F32), vmem((NX, NY, 16, virtuals), F32),
-        vmem((NX, NY, 16, virtuals), F32),
+        vmem((NX, 2, NY, 64, 128), F32), vmem((NX, NY, 64, 128), F32), vmem((NX, NY, 64, 128), F32),
+        vmem((NX, NY, 64, 128), F32),
         vmem((NZ, NY, 8, 128), F32), vmem((NZ, NY, 8, 128), F32), vmem((NY, 8, 128), F32),
         vmem((2 * NY, 8, 128), F32), vmem((8, 128), F32), vmem((vir_local, virtuals), F32),
         vmem((2, 8, 128), F32), vmem((8, 128), F32), vmem((8, 128), F32),
+        vmem((vir_local, aux), F32), dma((4,)), dma((1,)), dma((1,)),
         dma((2,)), dma((8,)), dma((8,)), dma((8,)), dma((8,)),
         dma((4,)), dma((4,)), dma((4,)), dma((4,)), dma((4,)), dma((4,)), dma((2,)), dma((2,)),
         dma((4,)), dma((4,)), dma((4,)), dma((4,)), dma((8,)), dma((8,)), dma((8,)), dma((8,)),
         dma((8,)), dma((8,)), dma((4,)), dma((4,)),
     ]
-    any_space = pl.BlockSpec(memory_space=pl.ANY)
+    in_hbm = pl.BlockSpec(memory_space=pltpu.HBM)
     in_vmem = pl.BlockSpec(memory_space=pltpu.VMEM)
     density, energy = pl.pallas_call(
         functools.partial(kernel, n_wide, dens_scale),
@@ -353,7 +431,7 @@
             jax.ShapeDtypeStruct((vir_local, virtuals), F32),
             jax.ShapeDtypeStruct((8, 128), F32),
         ),
-        in_specs=[any_space, any_space, in_vmem, in_vmem],
+        in_specs=[in_hbm, in_hbm, in_vmem, in_vmem],
         out_specs=(in_vmem, in_vmem),
         scratch_shapes=scratch,
         compiler_params=pltpu.CompilerParams(

time: 138 us -> 119 us (0.86)
  Pallas kernels: 132 us -> 112 us
    pallas_call x1, Pallas kernels: 132 us -> 112 us  [on_device(): pl.pallas_call(functools.partial(kernel, n_wide, dens_scale), out_shape=(...]
where the time goes in v2:
time: 119 us; the launch traced here: 118 us
  Pallas kernels  112 us (94%)
  local copies, waits for them, and re-layouts  4.29 us (4%)
  between operations  1.93 us (2%)
    pallas_call x1, Pallas kernels, on_device(): pl.pallas_call(functools.partial(kernel, n_wide, dens_scale), out_shape=(...  112 us
    unnamed x7, local copies, waits for them, and re-layouts  3.71 us

profile of v2, /device:TPU:8, one launch (start us, length us, event | category | flops | bytes accessed | tf_op | source)
XLA Modules:
  0.0 118.4 jit_solution(11418890935572327059)
XLA Ops:
  1.9 0.1 maximum_bitcast_fusion
  2.0 0.1 broadcast_in_dim.12.side
  2.1 0.0 copy-start
  2.1 1.4 %copy-done = f32[8,64,768]{2,1,0:T(8,128)S(1)} copy-done((f32[8,64,768]{2,1,0:T(8,128)S(1)}, f32[8,64,768]{2,1,0:T(8,128)}, u32[]{:S(2)}) %copy-start) | copy-done | bytes 1572888
  3.5 0.0 copy-start.1
  3.5 1.0 copy-done.1
  4.4 0.0 copy-start.2
  4.4 0.7 copy-done.2
  5.1 112.1 %pair_density.1 = (f32[64,512]{1,0:T(8,128)S(1)}, f32[8,128]{1,0:T(8,128)S(1)}) custom-call(f32[8,64,768]{2,1,0:T(8,128)S(1)} %copy-done, f32[96,768]{1,0:T(8,128)S(1)} %copy-done.1, f32[2,8,128]{2,1,0:T(8,128)S(1)} %broadcast_in_dim.12.side, f32[1,512]{1,0:T(1,128)S(1)} %bitcast.7), custom_call_target="tpu_custom_call" | custom-call | tf_op jit(solution)/shard_map/pair_density/pallas_call | solution.py:428
  117.2 0.5 slice.3
  117.7 0.7 copy.10
Async XLA Ops:
  2.1 1.4 %copy-start = (f32[8,64,768]{2,1,0:T(8,128)S(1)}, f32[8,64,768]{2,1,0:T(8,128)}, u32[]{:S(2)}) copy-start(f32[8,64,768]{2,1,0:T(8,128)} %raw.1) | copy-start | bytes 4718596
  3.5 1.0 copy-start.1
  4.4 0.7 copy-start.2

commit v3 on v2

--- a/solution.py
+++ b/solution.py
@@ -14,8 +14,8 @@
 NX, NZ, NY, NARROW = 4, 8, 4, 8
 PLANE = NX * NZ
 LAST, FIRST = PLANE - 1, 0
-UP_COLUMNS = (24, 7, 25, 6)
-DOWN_COLUMNS = (23, 8, 16, 15)
+UP_COLUMNS = ((24, 3, None), (6, 1, 0), (30, 1, 1), (26, 0, 0), (2, 0, 1), (4, 2, 0), (28, 2, 1))
+DOWN_COLUMNS = tuple((LAST - column, j, core) for column, j, core in UP_COLUMNS)
 
 
 def split(value):
@@ -40,7 +40,7 @@
     side_in, pv_own, pv_in,
     relay_buf, b_s, b_r, r_s,
     loc_sem, a_s, a_r, f_s, f_r, m1_s, m1_r, m2_s, m2_r, m3_s, m3_r, side_sem, pv_sem,
-    c_s, c_r, xs_s, xs_r, zs_s, zs_r, ys_s, ys_r, gz_s, gz_r, gx_s, gx_r,
+    c_s, c_r, xs_s, xs_r, zs_s, zs_r, ys_s, ys_r, gz_s, gz_r,
 ):
     w = lax.axis_index("wide")
     n = lax.axis_index("narrow")
@@ -71,8 +71,9 @@
 
     peers = [(w, (n + d) % NARROW) for d in range(1, NARROW)]
     peers += [at_y(d) for d in range(1, 2 * NY)]
-    peers += [(at_x(d), n) for d in range(1, NX)]
-    peers += [(at_z(d), n) for d in range(1, NZ)]
+    peers += [
+        (hi * PLANE + ((x + d // NZ) % NX) * NZ + (z + d % NZ) % NZ, n) for d in range(1, PLANE)
+    ]
     peers += [(up, n), (down, n)]
     barrier = pltpu.get_barrier_semaphore()
 
@@ -83,31 +84,32 @@
         greet(*peer)
     routes = ((LAST, FIRST, 0, UP_COLUMNS), (FIRST, LAST, 1, DOWN_COLUMNS))
     sends_on = jnp.logical_not(((plane == LAST) & (c == 0)) | ((plane == FIRST) & (c == 1)))
+    def takes(core):
+        return c == c if core is None else c == core
+
     for source, target, parity, columns in routes:
-        @pl.when(plane == source)
-        def _():
-            for column in columns:
+        for column, j, core in columns:
+            @pl.when((plane == source) & takes(core))
+            def _():
                 greet(hi * PLANE + column, n)
 
-        for j, column in enumerate(columns):
-            @pl.when(plane == column)
+            @pl.when((plane == column) & takes(core))
             def _():
                 greet(hi * PLANE + source, n)
                 greet((1 - hi) * PLANE + target, 2 * ((j + NY - y) % NY) + parity)
 
-        @pl.when((plane == target) & (c == parity))
-        def _():
-            for j, column in enumerate(columns):
-                for core in range(2):
-                    greet((1 - hi) * PLANE + column, 2 * ((j + NY - y) % NY) + core)
+            @pl.when((plane == target) & (c == parity))
+            def _():
+                for from_core in (0, 1) if core is None else (core,):
+                    greet((1 - hi) * PLANE + column, 2 * ((j + NY - y) % NY) + from_core)
 
     at_end = (plane == LAST) | (plane == FIRST)
-    on_way = plane == UP_COLUMNS[0]
-    for column in UP_COLUMNS[1:] + DOWN_COLUMNS:
-        on_way = on_way | (plane == column)
+    on_way = plane < 0
+    for column, j, core in UP_COLUMNS + DOWN_COLUMNS:
+        on_way = on_way | ((plane == column) & takes(core))
     for case, more in (
-        (at_end & sends_on, 3 * len(UP_COLUMNS)),
-        (at_end & jnp.logical_not(sends_on), len(UP_COLUMNS)),
+        (at_end & sends_on, NY + NARROW),
+        (at_end & jnp.logical_not(sends_on), NY),
         (on_way, 2),
         (jnp.logical_not(at_end | on_way), 0),
     ):
@@ -116,24 +118,30 @@
             pl.semaphore_wait(barrier, len(peers) + more)
 
     rows_q = metric.shape[0] // NX
-    own_rows = pl.ds(x * (NY * rows_q) + y * rows_q, rows_q)
+    half_aux = metric.shape[1] // 2
+    block = NY * rows_q
+    half = NX * block
+    mine = z % 2
+
+    def aux_half(piece):
+        return pl.ds(pl.multiple_of(piece * half_aux, half_aux), half_aux)
+
+    share = metric.at[pl.ds(x * rows_q, rows_q), aux_half(mine)]
+    own_part = mbuf.at[pl.ds(x * block + y * rows_q, rows_q), aux_half(mine)]
     m1 = []
     for d in range(1, NY):
-        copy = remote(
-            metric.at[pl.ds(x * rows_q, rows_q)], mbuf.at[own_rows],
-            m1_s.at[d], m1_r.at[d], w, 2 * ((y + d) % NY) + c,
-        )
+        copy = remote(share, own_part, m1_s.at[d], m1_r.at[d], w, 2 * ((y + d) % NY) + c)
         copy.start()
         m1.append(copy)
-    m_local = pltpu.make_async_copy(metric.at[pl.ds(x * rows_q, rows_q)], mbuf.at[own_rows], loc_sem.at[0])
+    m_local = pltpu.make_async_copy(share, own_part, loc_sem.at[0])
     m_local.start()
     side_copy = remote(side, side_in, side_sem.at[0], side_sem.at[1], fwd, n)
     side_copy.start()
 
     for source, target, parity, columns in routes:
-        @pl.when(plane == source)
-        def _():
-            for j, column in enumerate(columns):
+        for column, j, core in columns:
+            @pl.when((plane == source) & takes(core))
+            def _():
                 k = (j + NY - y) % NY
                 remote(
                     raw.at[2 * k + parity], relay_buf, b_s.at[j], b_r.at[0], hi * PLANE + column, n
@@ -170,8 +178,8 @@
         )
 
     for source, target, parity, columns in routes:
-        for j, column in enumerate(columns):
-            @pl.when(plane == column)
+        for column, j, core in columns:
+            @pl.when((plane == column) & takes(core))
             def _():
                 remote(raw.at[0], relay_buf, b_s.at[j], b_r.at[0], hi * PLANE + source, n).wait_recv()
                 second_leg(target, parity, j).start()
@@ -179,18 +187,29 @@
     m_local.wait()
     for copy in m1:
         copy.wait_recv()
-    block = NY * rows_q
-    half = NX * block
-    m2 = []
-    for d in range(1, NX):
-        rows = pl.ds(x * block, block)
-        copy = remote(mbuf.at[rows], mbuf.at[rows], m2_s.at[d], m2_r.at[d], at_x(d), n)
-        copy.start()
-        m2.append(copy)
+
+    def m_piece(which, piece):
+        return mbuf.at[pl.ds(which * block, block), aux_half(piece)]
+
+    def around_x(way, piece):
+        src = m_piece(x, piece)
+        k = 2 * way + piece
+        return remote(src, src, m2_s.at[k], m2_r.at[k], at_x(1 - 2 * way + NX), n)
+
+    def on_around_x(way):
+        src = m_piece((x + NX - 1 + 2 * way) % NX, way)
+        return remote(src, src, m2_s.at[4 + way], m2_r.at[4 + way], at_x(1 - 2 * way + NX), n)
+
+    m_z = remote(
+        m_piece(x, mine), m_piece(x, mine), m1_s.at[0], m1_r.at[0], hi * PLANE + x * NZ + z + 1 - 2 * mine, n
+    )
+    m_z.start()
+    for way in (0, 1):
+        around_x(way, mine).start()
     m3 = []
 
     def to_partner(d):
-        which = (x + NX - d) % NX
+        which = (x + d) % NX
         copy = remote(
             mbuf.at[pl.ds(which * block, block)], mbuf.at[pl.ds(half + which * block, block)],
             m3_s.at[d], m3_r.at[d], w, 2 * y + 1 - c,
@@ -198,22 +217,32 @@
         copy.start()
         m3.append(copy)
 
-    to_partner(0)
-
     side_copy.wait()
     virtuals = vir.shape[1]
-    rinv[...] = jnp.broadcast_to(vir[...], (virtuals, virtuals))
+    pbuf[...] = jnp.broadcast_to(vir[...], (virtuals, virtuals))
     energies = side[0][:1, :1] + side_in[0][:1, :1]
     for r in range(0, virtuals, 128):
-        across = rinv[:, r:r + 128].T
-        pbuf[r:r + 128, :] = 1.0 / ((rinv[r:r + 128, :] + across) - energies)
-
-    for d in (2, 3, 4):
+        across = pbuf[:, r:r + 128].T
+        rinv[r:r + 128, :] = 1.0 / ((pbuf[r:r + 128, :] + across) - energies)
+
+    m_z.wait_recv()
+    for way in (0, 1):
+        around_x(way, 1 - mine).start()
+    to_partner(0)
+    for d in (2, 3):
         a2a[d].wait_recv()
         forward(d)
-    for d in range(1, NX):
-        m2[d - 1].wait_recv()
-        to_partner(d)
+    for way in (0, 1):
+        around_x(way, way).wait_recv()
+        on_around_x(way).start()
+    a2a[4].wait_recv()
+    forward(4)
+    for way in (0, 1):
+        around_x(way, 1 - way).wait_recv()
+        to_partner(3 - 2 * way)
+    for way in (0, 1):
+        on_around_x(way).wait_recv()
+    to_partner(2)
     a2a[5].wait_recv()
     forward(5)
     for copy in m3:
@@ -242,36 +271,42 @@
 
         lax.fori_loop(0, mbuf.shape[0] // 256, tile, 0)
 
-    for d in (6, 7):
-        a2a[d].wait_recv()
-        forward(d)
     own_slot.wait()
     fit(rbuf, fi_hi, fi_lo, slots[:4])
-    fit(rbuf, fi_hi, fi_lo, slots[4:])
+    a2a[6].wait_recv()
+    forward(6)
     for d in range(4):
         forwards[d].wait_recv()
     fit(jbuf, fj_hi, fj_lo, slots[:4])
+    a2a[7].wait_recv()
+    forward(7)
+    fit(rbuf, fi_hi, fi_lo, slots[4:])
+
+    def pair_rows(four):
+        for k, slot in enumerate(four):
+            part = pl.ds(k * 64, 64)
+            x_hi[part, :] = fj_hi[slot]
+            x_lo[part, :] = fj_lo[slot]
+
+        def tile(cb, carry):
+            four_b = pl.ds(cb * 4, 4)
+            shape = (256, fi_hi.shape[2])
+            ints = dot3(x_hi[...], x_lo[...], fi_hi[four_b].reshape(shape), fi_lo[four_b].reshape(shape))
+            cols = pl.ds(pl.multiple_of(cb * 256, 256), 256)
+            for k, slot in enumerate(four):
+                rows = pl.ds(pl.multiple_of(slot * 64, 64), 64)
+                part = ints[k * 64:(k + 1) * 64]
+                pbuf[rows, cols] = part
+                abuf[rows, cols] = part * rinv[rows, cols]
+            return carry
+
+        lax.fori_loop(0, 2, tile, 0)
+
+    pair_rows(slots[:4])
     for d in range(4, 8):
         forwards[d].wait_recv()
     fit(jbuf, fj_hi, fj_lo, slots[4:])
-
-    rinv[...] = pbuf[...]
-
-    def pair_tile(t, carry):
-        ra, cb = t // 2, t % 2
-        four_a, four_b = pl.ds(ra * 4, 4), pl.ds(cb * 4, 4)
-        shape = (256, fi_hi.shape[2])
-        ints = dot3(
-            fi_hi[four_a].reshape(shape), fi_lo[four_a].reshape(shape),
-            fj_hi[four_b].reshape(shape), fj_lo[four_b].reshape(shape),
-        )
-        rows = pl.ds(pl.multiple_of(ra * 256, 256), 256)
-        cols = pl.ds(pl.multiple_of(cb * 256, 256), 256)
-        pbuf[rows, cols] = ints
-        abuf[rows, cols] = ints * rinv[rows, cols]
-        return carry
-
-    lax.fori_loop(0, 4, pair_tile, 0)
+    pair_rows(slots[4:])
 
     def value_tile(t, total):
         ra, cb = t // 2, t % 2
@@ -358,32 +393,27 @@
     rows = pl.ds(pl.multiple_of(z * 8, 8), 8)
     cols = pl.ds(pl.multiple_of(x * 128, 128), 128)
     gz = []
-    for d in range(1, NZ):
-        copy = remote(tbuf, ofull.at[rows, cols], gz_s.at[d], gz_r.at[d], at_z(d), n)
+    for d in range(1, PLANE):
+        copy = remote(
+            tbuf, ofull.at[rows, cols], gz_s.at[d], gz_r.at[d],
+            hi * PLANE + ((x + d // NZ) % NX) * NZ + (z + d % NZ) % NZ, n,
+        )
         copy.start()
         gz.append(copy)
     ofull[rows, cols] = sum_y
-    for copy in gz:
-        copy.wait_recv()
-    gx = []
-    for d in range(1, NX):
-        copy = remote(ofull.at[:, cols], ofull.at[:, cols], gx_s.at[d], gx_r.at[d], at_x(d), n)
-        copy.start()
-        gx.append(copy)
     pv_copy.wait()
     energy_out[...] = pv_own[...] + pv_in[...]
-    for copy in gx:
+    for copy in gz:
         copy.wait_recv()
     dens_out[...] = ofull[...]
 
     for source, target, parity, columns in routes:
-        @pl.when(plane == source)
-        def _():
-            for j, column in enumerate(columns):
+        for column, j, core in columns:
+            @pl.when((plane == source) & takes(core))
+            def _():
                 remote(raw.at[0], relay_buf, b_s.at[j], b_r.at[0], hi * PLANE + column, n).wait_send()
 
-        for j, column in enumerate(columns):
-            @pl.when(plane == column)
+            @pl.when((plane == column) & takes(core))
             def _():
                 second_leg(target, parity, j).wait_send()
 
@@ -392,7 +422,12 @@
         for copy in forwards:
             copy.wait_send()
 
-    for copy in m1 + m2 + m3 + a2a[1:] + core_copies + x_copies + z_copies + y_copies + gz + gx:
+    for way in (0, 1):
+        on_around_x(way).wait_send()
+        for piece in (0, 1):
+            around_x(way, piece).wait_send()
+
+    for copy in m1 + [m_z] + m3 + a2a[1:] + core_copies + x_copies + z_copies + y_copies + gz:
         copy.wait_send()
 
 
@@ -419,9 +454,9 @@
         vmem((2, 8, 128), F32), vmem((8, 128), F32), vmem((8, 128), F32),
         vmem((vir_local, aux), F32), dma((4,)), dma((1,)), dma((1,)),
         dma((2,)), dma((8,)), dma((8,)), dma((8,)), dma((8,)),
-        dma((4,)), dma((4,)), dma((4,)), dma((4,)), dma((4,)), dma((4,)), dma((2,)), dma((2,)),
+        dma((4,)), dma((4,)), dma((6,)), dma((6,)), dma((4,)), dma((4,)), dma((2,)), dma((2,)),
         dma((4,)), dma((4,)), dma((4,)), dma((4,)), dma((8,)), dma((8,)), dma((8,)), dma((8,)),
-        dma((8,)), dma((8,)), dma((4,)), dma((4,)),
+        dma((32,)), dma((32,)),
     ]
     in_hbm = pl.BlockSpec(memory_space=pltpu.HBM)
     in_vmem = pl.BlockSpec(memory_space=pltpu.VMEM)

time: 119 us -> 113 us (0.950)
  Pallas kernels: 112 us -> 107 us
    pallas_call x1, Pallas kernels: 112 us -> 107 us  [on_device(): pl.pallas_call(functools.partial(kernel, n_wide, dens_scale), out_shape=(...]
where the time goes in v3:
time: 113 us
  Pallas kernels  107 us (95%)
  local copies, waits for them, and re-layouts  4.29 us (4%)
  between operations  1.93 us (2%)
    pallas_call x1, Pallas kernels, on_device(): pl.pallas_call(functools.partial(kernel, n_wide, dens_scale), out_shape=(...  107 us
    unnamed x7, local copies, waits for them, and re-layouts  3.71 us

profile of v3, /device:TPU:8, one launch (start us, length us, event | category | flops | bytes accessed | tf_op | source)
XLA Modules:
  0.0 112.9 jit_solution(5831222946384076046)
XLA Ops:
  1.9 0.1 maximum_bitcast_fusion
  2.0 0.1 broadcast_in_dim.12.side
  2.1 0.0 copy-start
  2.1 1.4 %copy-done = f32[8,64,768]{2,1,0:T(8,128)S(1)} copy-done((f32[8,64,768]{2,1,0:T(8,128)S(1)}, f32[8,64,768]{2,1,0:T(8,128)}, u32[]{:S(2)}) %copy-start) | copy-done | bytes 1572888
  3.5 0.0 copy-start.1
  3.5 1.0 copy-done.1
  4.4 0.0 copy-start.2
  4.4 0.7 copy-done.2
  5.1 106.6 %pair_density.1 = (f32[64,512]{1,0:T(8,128)S(1)}, f32[8,128]{1,0:T(8,128)S(1)}) custom-call(f32[8,64,768]{2,1,0:T(8,128)S(1)} %copy-done, f32[96,768]{1,0:T(8,128)S(1)} %copy-done.1, f32[2,8,128]{2,1,0:T(8,128)S(1)} %broadcast_in_dim.12.side, f32[1,512]{1,0:T(1,128)S(1)} %bitcast.7), custom_call_target="tpu_custom_call" | custom-call | tf_op jit(solution)/shard_map/pair_density/pallas_call | solution.py:463
  111.7 0.5 slice.3
  112.2 0.7 copy.10
Async XLA Ops:
  2.1 1.4 %copy-start = (f32[8,64,768]{2,1,0:T(8,128)S(1)}, f32[8,64,768]{2,1,0:T(8,128)}, u32[]{:S(2)}) copy-start(f32[8,64,768]{2,1,0:T(8,128)} %raw.1) | copy-start | bytes 4718596
  3.5 1.0 copy-start.1
  4.4 0.7 copy-start.2

commit v4 on v3

--- a/solution.py
+++ b/solution.py
@@ -225,26 +225,28 @@
         across = pbuf[:, r:r + 128].T
         rinv[r:r + 128, :] = 1.0 / ((pbuf[r:r + 128, :] + across) - energies)
 
-    m_z.wait_recv()
-    for way in (0, 1):
-        around_x(way, 1 - mine).start()
-    to_partner(0)
     for d in (2, 3):
         a2a[d].wait_recv()
         forward(d)
+    m_z.wait_recv()
+    for way in (0, 1):
+        around_x(way, 1 - mine).start()
+    to_partner(0)
+    a2a[4].wait_recv()
+    forward(4)
     for way in (0, 1):
         around_x(way, way).wait_recv()
         on_around_x(way).start()
-    a2a[4].wait_recv()
-    forward(4)
+    a2a[5].wait_recv()
+    forward(5)
     for way in (0, 1):
         around_x(way, 1 - way).wait_recv()
         to_partner(3 - 2 * way)
     for way in (0, 1):
         on_around_x(way).wait_recv()
     to_partner(2)
-    a2a[5].wait_recv()
-    forward(5)
+    a2a[6].wait_recv()
+    forward(6)
     for copy in m3:
         copy.wait_recv()
 
@@ -272,14 +274,12 @@
         lax.fori_loop(0, mbuf.shape[0] // 256, tile, 0)
 
     own_slot.wait()
+    a2a[7].wait_recv()
+    forward(7)
     fit(rbuf, fi_hi, fi_lo, slots[:4])
-    a2a[6].wait_recv()
-    forward(6)
     for d in range(4):
         forwards[d].wait_recv()
     fit(jbuf, fj_hi, fj_lo, slots[:4])
-    a2a[7].wait_recv()
-    forward(7)
     fit(rbuf, fi_hi, fi_lo, slots[4:])
 
     def pair_rows(four):
@@ -470,7 +470,7 @@
         out_specs=(in_vmem, in_vmem),
         scratch_shapes=scratch,
         compiler_params=pltpu.CompilerParams(
-            collective_id=0, has_side_effects=True, vmem_limit_bytes=48 << 20
+            collective_id=0, has_side_effects=True, vmem_limit_bytes=55500000
         ),
         name="pair_density",
     )(raw_ints, metric, side, vir_energy[None, :])

time: 113 us -> 108 us (0.956)
  the two profiles are of different devices: /device:TPU:8 before, /device:TPU:6 now
where the time goes in v4:
time: 108 us
  Pallas kernels  103 us (95%)
  local copies, waits for them, and re-layouts  2.89 us (3%)
  between operations  1.93 us (2%)
    pallas_call x1, Pallas kernels, on_device(): pl.pallas_call(functools.partial(kernel, n_wide, dens_scale), out_shape=(...  103 us
    unnamed x5, local copies, waits for them, and re-layouts  2.3 us

profile of v4, /device:TPU:6, one launch (start us, length us, event | category | flops | bytes accessed | tf_op | source)
XLA Modules:
  0.0 108.0 jit_solution(344355417441207988)
XLA Ops:
  1.9 0.1 maximum_bitcast_fusion
  2.0 0.1 broadcast_in_dim.12.side
  2.1 0.0 copy-start
  2.1 1.0 copy-done
  3.0 0.0 copy-start.1
  3.0 0.7 copy-done.1
  3.7 103.1 %pair_density.1 = (f32[64,512]{1,0:T(8,128)S(1)}, f32[8,128]{1,0:T(8,128)S(1)}) custom-call(f32[8,64,768]{2,1,0:T(8,128)} %raw.1, f32[96,768]{1,0:T(8,128)S(1)} %copy-done, f32[2,8,128]{2,1,0:T(8,128)S(1)} %broadcast_in_dim.12.side, f32[1,512]{1,0:T(1,128)S(1)} %bitcast.7), custom_call_target="tpu_custom_call" | custom-call | tf_op jit(solution)/shard_map/pair_density/pallas_call | solution.py:463
  106.8 0.5 slice.3
  107.3 0.7 copy.10
Async XLA Ops:
  2.1 1.0 copy-start
  3.0 0.7 copy-start.1

commit v5 on v4

--- a/solution.py
+++ b/solution.py
@@ -14,7 +14,7 @@
 NX, NZ, NY, NARROW = 4, 8, 4, 8
 PLANE = NX * NZ
 LAST, FIRST = PLANE - 1, 0
-UP_COLUMNS = ((24, 3, None), (6, 1, 0), (30, 1, 1), (26, 0, 0), (2, 0, 1), (4, 2, 0), (28, 2, 1))
+UP_COLUMNS = ((7, 3, None), (25, 1, 0), (1, 1, 1), (5, 0, 0), (29, 0, 1), (27, 2, 0), (3, 2, 1))
 DOWN_COLUMNS = tuple((LAST - column, j, core) for column, j, core in UP_COLUMNS)
 
 
@@ -148,11 +148,16 @@
                 ).start()
 
     a2a = [None]
+    parts = [pl.ds(0, raw.shape[1] // 2), pl.ds(raw.shape[1] // 2, raw.shape[1] // 2)]
     for d in range(1, NARROW):
         to = (n + d) % NARROW
-        copy = remote(raw.at[to], rbuf.at[n], a_s.at[d], a_r.at[d], w, to)
-        copy.start()
-        a2a.append(copy)
+        pair = [
+            remote(raw.at[to, part], rbuf.at[n, part], a_s.at[2 * d + h], a_r.at[2 * d + h], w, to)
+            for h, part in enumerate(parts)
+        ]
+        for copy in pair:
+            copy.start()
+        a2a.append(pair)
     own_slot = pltpu.make_async_copy(raw.at[n], rbuf.at[n], loc_sem.at[1])
     own_slot.start()
     slots = [(n + NARROW - d) % NARROW for d in range(NARROW)]
@@ -160,29 +165,39 @@
 
     def forward(d):
         src = raw.at[n] if d == 0 else rbuf.at[slots[d]]
-        copy = remote(src, jbuf.at[slots[d]], f_s.at[d], f_r.at[d], fwd, n)
-        forwards.append(copy)
-
-        @pl.when(sends_on)
-        def _():
-            copy.start()
+        pair = [
+            remote(src.at[part], jbuf.at[slots[d], part], f_s.at[2 * d + h], f_r.at[2 * d + h], fwd, n)
+            for h, part in enumerate(parts)
+        ]
+        forwards.append(pair)
+        for h in range(2):
+            if d:
+                a2a[d][h].wait_recv()
+
+            @pl.when(sends_on)
+            def _():
+                pair[h].start()
 
     forward(0)
-    a2a[1].wait_recv()
     forward(1)
 
     def second_leg(target, parity, j):
         to = 2 * ((j + NY - y) % NY) + parity
-        return remote(
-            relay_buf, jbuf.at[n], r_s.at[0], f_r.at[(to + NARROW - n) % NARROW], (1 - hi) * PLANE + target, to
-        )
+        d = (to + NARROW - n) % NARROW
+        return [
+            remote(
+                relay_buf.at[part], jbuf.at[n, part], r_s.at[h], f_r.at[2 * d + h], (1 - hi) * PLANE + target, to
+            )
+            for h, part in enumerate(parts)
+        ]
 
     for source, target, parity, columns in routes:
         for column, j, core in columns:
             @pl.when((plane == column) & takes(core))
             def _():
                 remote(raw.at[0], relay_buf, b_s.at[j], b_r.at[0], hi * PLANE + source, n).wait_recv()
-                second_leg(target, parity, j).start()
+                for copy in second_leg(target, parity, j):
+                    copy.start()
 
     m_local.wait()
     for copy in m1:
@@ -226,18 +241,15 @@
         rinv[r:r + 128, :] = 1.0 / ((pbuf[r:r + 128, :] + across) - energies)
 
     for d in (2, 3):
-        a2a[d].wait_recv()
         forward(d)
     m_z.wait_recv()
     for way in (0, 1):
         around_x(way, 1 - mine).start()
     to_partner(0)
-    a2a[4].wait_recv()
     forward(4)
     for way in (0, 1):
         around_x(way, way).wait_recv()
         on_around_x(way).start()
-    a2a[5].wait_recv()
     forward(5)
     for way in (0, 1):
         around_x(way, 1 - way).wait_recv()
@@ -245,7 +257,6 @@
     for way in (0, 1):
         on_around_x(way).wait_recv()
     to_partner(2)
-    a2a[6].wait_recv()
     forward(6)
     for copy in m3:
         copy.wait_recv()
@@ -274,11 +285,11 @@
         lax.fori_loop(0, mbuf.shape[0] // 256, tile, 0)
 
     own_slot.wait()
-    a2a[7].wait_recv()
     forward(7)
     fit(rbuf, fi_hi, fi_lo, slots[:4])
     for d in range(4):
-        forwards[d].wait_recv()
+        for copy in forwards[d]:
+            copy.wait_recv()
     fit(jbuf, fj_hi, fj_lo, slots[:4])
     fit(rbuf, fi_hi, fi_lo, slots[4:])
 
@@ -304,7 +315,8 @@
 
     pair_rows(slots[:4])
     for d in range(4, 8):
-        forwards[d].wait_recv()
+        for copy in forwards[d]:
+            copy.wait_recv()
     fit(jbuf, fj_hi, fj_lo, slots[4:])
     pair_rows(slots[4:])
 
@@ -415,19 +427,21 @@
 
             @pl.when((plane == column) & takes(core))
             def _():
-                second_leg(target, parity, j).wait_send()
+                for copy in second_leg(target, parity, j):
+                    copy.wait_send()
 
     @pl.when(sends_on)
     def _():
-        for copy in forwards:
-            copy.wait_send()
+        for pair in forwards:
+            for copy in pair:
+                copy.wait_send()
 
     for way in (0, 1):
         on_around_x(way).wait_send()
         for piece in (0, 1):
             around_x(way, piece).wait_send()
 
-    for copy in m1 + [m_z] + m3 + a2a[1:] + core_copies + x_copies + z_copies + y_copies + gz:
+    for copy in m1 + [m_z] + m3 + sum(a2a[1:], []) + core_copies + x_copies + z_copies + y_copies + gz:
         copy.wait_send()
 
 
@@ -452,8 +466,8 @@
         vmem((NZ, NY, 8, 128), F32), vmem((NZ, NY, 8, 128), F32), vmem((NY, 8, 128), F32),
         vmem((2 * NY, 8, 128), F32), vmem((8, 128), F32), vmem((vir_local, virtuals), F32),
         vmem((2, 8, 128), F32), vmem((8, 128), F32), vmem((8, 128), F32),
-        vmem((vir_local, aux), F32), dma((4,)), dma((1,)), dma((1,)),
-        dma((2,)), dma((8,)), dma((8,)), dma((8,)), dma((8,)),
+        vmem((vir_local, aux), F32), dma((4,)), dma((1,)), dma((2,)),
+        dma((2,)), dma((16,)), dma((16,)), dma((16,)), dma((16,)),
         dma((4,)), dma((4,)), dma((6,)), dma((6,)), dma((4,)), dma((4,)), dma((2,)), dma((2,)),
         dma((4,)), dma((4,)), dma((4,)), dma((4,)), dma((8,)), dma((8,)), dma((8,)), dma((8,)),
         dma((32,)), dma((32,)),

time: 108 us -> 107 us (level)
  the two profiles are of different devices: /device:TPU:6 before, /device:TPU:8 now
where the time goes in v5:
time: 107 us
  Pallas kernels  102 us (95%)
  local copies, waits for them, and re-layouts  2.89 us (3%)
  between operations  1.93 us (2%)
    pallas_call x1, Pallas kernels, on_device(): pl.pallas_call(functools.partial(kernel, n_wide, dens_scale), out_shape=(...  102 us
    unnamed x5, local copies, waits for them, and re-layouts  2.3 us

profile of v5, /device:TPU:8, one launch (start us, length us, event | category | flops | bytes accessed | tf_op | source)
XLA Modules:
  0.0 106.5 jit_solution(4548843665044704960)
XLA Ops:
  1.9 0.1 maximum_bitcast_fusion
  2.0 0.1 broadcast_in_dim.12.side
  2.1 0.0 copy-start
  2.1 1.0 copy-done
  3.0 0.0 copy-start.1
  3.0 0.7 copy-done.1
  3.7 101.7 %pair_density.1 = (f32[64,512]{1,0:T(8,128)S(1)}, f32[8,128]{1,0:T(8,128)S(1)}) custom-call(f32[8,64,768]{2,1,0:T(8,128)} %raw.1, f32[96,768]{1,0:T(8,128)S(1)} %copy-done, f32[2,8,128]{2,1,0:T(8,128)S(1)} %broadcast_in_dim.12.side, f32[1,512]{1,0:T(1,128)S(1)} %bitcast.7), custom_call_target="tpu_custom_call" | custom-call | tf_op jit(solution)/shard_map/pair_density/pallas_call | solution.py:477
  105.4 0.5 slice.3
  105.9 0.7 copy.10
Async XLA Ops:
  2.1 1.0 copy-start
  3.0 0.7 copy-start.1
